TPU v7x, 32 devices: a whole 2x2x4 slice. The times are simulated.
32 devices in a mesh: section: 4 (over y, x), expert: 8 (over z, core).
Axes of the slice: x: 2, y: 2, z: 4, core: 2. Of those that a mesh axis runs over, the one named last changes fastest.
Arguments:
- saved_inputs: bfloat16 [4, 2, 96, 3072], P('section', None, 'expert'), may hold values from -6 to 6
- expert_ids: int32 [4, 2, 96, 2], P('section'), may hold values from 0 to 3, all different within a row; in each aligned block of 12 rows (0 to 11, 12 to 23, ..., all dimensions but the last counted through in order) at most 9 rows name the same one
- combine: bfloat16 [4, 2, 96, 2], P('section'), may hold values from 0.19921875 to 1
- top_grad: bfloat16 [2, 96, 3072], P(None, 'expert'), may hold values from -6 to 6
- w_gate: bfloat16 [4, 3072, 32768], P('section', None, 'expert'), may hold values from -0.109375 to 0.109375
- w_up: bfloat16 [4, 3072, 32768], P('section', None, 'expert'), may hold values from -0.109375 to 0.109375
- w_down: bfloat16 [4, 32768, 3072], P('section', 'expert'), may hold values from -0.0625 to 0.0625
Outputs:
- input_grads: bfloat16 [4, 2, 96, 3072], P('section', None, 'expert')
- combine_grads: float32 [4, 2, 96, 2], P('section', None, 'expert')
Inputs may be any that keep to these rules, and one draw needn't show every extreme that they name: `expert_ids`: each token names 2 different experts. Among the 12 tokens of one index of expert in one layer and micro-batch, no expert is named more than 9 times, and some expert reaches 9.
All inputs are finite; a program needn't handle non-finite values.
Results may differ from a plain program's by a relative error of at most 0.018.
Values may be sent and summed in bfloat16 or wider, within the bound.
No kernel may reach another device: no remote copies, remote signals or barrier semaphores. Data moves between devices by JAX's collectives and lax.ppermute only.
A program may use at most 192 MiB of HBM per device.

v0:
```python
import jax
import jax.numpy as jnp
from jax import lax
from jax.sharding import PartitionSpec as P

EXPERTS = 4
CAP = 9


def shifted(shard, axis, by):
    length = lax.axis_size(axis)
    pairs = [(i, i + by) for i in range(length) if 0 <= i + by < length]
    return lax.ppermute(shard, axis, pairs)


def silu_parts(values):
    sig = jax.nn.sigmoid(values)
    return (values * sig, sig * (1.0 + values * (1.0 - sig)))


def slot_tables(chosen, experts, capacity):
    onehot = (chosen[:, :, None] == jnp.arange(experts, dtype=jnp.int32)).astype(jnp.int32)
    before = jnp.cumsum(onehot, axis=1) - onehot
    position = jnp.sum(before * onehot, axis=2)
    same_slot = (
        position[:, None, None, :] == jnp.arange(capacity, dtype=jnp.int32)[None, None, :, None]
    ).astype(jnp.int32)
    return (jnp.transpose(onehot, (0, 2, 1))[:, :, None, :] * same_slot).astype(jnp.float32)


def expert_grads(got_inputs, got_grads, weights, gate_part, lift_part, down_part):
    senders, capacity, width = got_inputs.shape
    inputs = got_inputs.reshape(senders * capacity, width)
    grads = got_grads.reshape(senders * capacity, width)
    pre_gate = jnp.dot(inputs, gate_part, preferred_element_type=jnp.float32)
    pre_lift = jnp.dot(inputs, lift_part, preferred_element_type=jnp.float32)
    hidden_grad = jnp.einsum("rd,fd->rf", grads, down_part, preferred_element_type=jnp.float32)
    active, slope = silu_parts(pre_gate)
    slot_grads = jnp.sum(hidden_grad * active * pre_lift, axis=-1)
    scaled = weights.reshape(-1)[:, None] * hidden_grad
    gate_grad = (scaled * pre_lift * slope).astype(jnp.bfloat16)
    lift_grad = (scaled * active).astype(jnp.bfloat16)
    moved = jnp.einsum("rf,df->rd", gate_grad, gate_part, preferred_element_type=jnp.float32)
    moved = moved + jnp.einsum(
        "rf,df->rd", lift_grad, lift_part, preferred_element_type=jnp.float32
    )
    return (moved.reshape(senders, capacity, width), slot_grads.reshape(senders, capacity))


def per_device(saved_inputs, expert_ids, combine, top_grad, w_gate, w_up, w_down):
    devices = lax.axis_size("expert")
    sections = lax.axis_size("section")
    my_index = lax.axis_index("expert")
    my_section = lax.axis_index("section")
    gate_part = w_gate[0]
    lift_part = w_up[0]
    down_part = w_down[0]
    micro = saved_inputs.shape[1]
    tokens = saved_inputs.shape[2]
    width = saved_inputs.shape[3]
    choose = expert_ids.shape[3]
    experts = EXPERTS
    capacity = CAP
    group = devices // experts
    own_expert = my_index // group
    grads_out = jnp.zeros(saved_inputs.shape[1:], jnp.bfloat16)
    slots_out = jnp.zeros((micro, tokens, choose), jnp.float32)
    passed = jnp.zeros((tokens, width), jnp.bfloat16)
    for step in range(micro + sections - 1):
        index = step - (sections - 1 - my_section)
        valid = (index >= 0) & (index < micro)
        current = jnp.clip(index, 0, micro - 1)
        inputs_now = lax.dynamic_index_in_dim(saved_inputs[0], current, 0, keepdims=False)
        from_top = lax.dynamic_index_in_dim(top_grad, current, 0, keepdims=False)
        upper = jnp.where(my_section == sections - 1, from_top, passed)
        chosen = lax.dynamic_index_in_dim(expert_ids[0], current, 0, keepdims=False).reshape(
            devices, tokens * choose
        )
        weights_all = (
            lax.dynamic_index_in_dim(combine[0], current, 0, keepdims=False)
            .reshape(devices, tokens * choose)
            .astype(jnp.float32)
        )
        tables = slot_tables(chosen, experts, capacity)
        recv_table = lax.dynamic_index_in_dim(tables, own_expert, 1, keepdims=False)
        recv_weights = jnp.einsum(
            "jcr,jr->jc", recv_table, weights_all, precision=lax.Precision.HIGHEST
        )
        send_table = lax.dynamic_index_in_dim(tables, my_index, 0, keepdims=False)
        place = jnp.sum(send_table.reshape(experts, capacity, tokens, choose), axis=3)
        place_half = place.astype(jnp.bfloat16)
        sent_inputs = jnp.einsum(
            "ect,td->ecd", place_half, inputs_now, preferred_element_type=jnp.float32
        ).astype(jnp.bfloat16)
        sent_grads = jnp.einsum(
            "ect,td->ecd", place_half, upper, preferred_element_type=jnp.float32
        ).astype(jnp.bfloat16)
        sent_inputs = jnp.repeat(sent_inputs, group, axis=0)
        sent_grads = jnp.repeat(sent_grads, group, axis=0)
        got_inputs, got_grads = (
            lax.all_to_all(sent_inputs, "expert", split_axis=0, concat_axis=0, tiled=True),
            lax.all_to_all(sent_grads, "expert", split_axis=0, concat_axis=0, tiled=True),
        )

        def active_case(first, second):
            return expert_grads(first, second, recv_weights, gate_part, lift_part, down_part)

        def empty_case(first, second):
            return (
                jnp.zeros((devices, capacity, width), jnp.float32),
                jnp.zeros((devices, capacity), jnp.float32),
            )

        part_moved, part_slots = lax.cond(valid, active_case, empty_case, got_inputs, got_grads)
        moved_half = part_moved.astype(jnp.bfloat16)
        slots_half = part_slots.astype(jnp.bfloat16)
        back_moved, back_slots = (
            lax.all_to_all(moved_half, "expert", split_axis=0, concat_axis=0, tiled=True),
            lax.all_to_all(slots_half, "expert", split_axis=0, concat_axis=0, tiled=True),
        )
        back_moved = jnp.sum(
            back_moved.astype(jnp.float32).reshape(experts, group, capacity, width), axis=1
        )
        back_slots = jnp.sum(
            back_slots.astype(jnp.float32).reshape(experts, group, capacity), axis=1
        )
        moved = jnp.einsum("ect,ecd->td", place, back_moved, precision=lax.Precision.HIGHEST)
        slot_grad = jnp.einsum(
            "ecr,ec->r", send_table, back_slots, precision=lax.Precision.HIGHEST
        ).reshape(tokens, choose)
        result = (upper.astype(jnp.float32) + moved).astype(jnp.bfloat16)
        old_grad = lax.dynamic_index_in_dim(grads_out, current, 0, keepdims=False)
        grads_out = lax.dynamic_update_index_in_dim(
            grads_out, jnp.where(valid, result, old_grad), current, 0
        )
        old_slots = lax.dynamic_index_in_dim(slots_out, current, 0, keepdims=False)
        slots_out = lax.dynamic_update_index_in_dim(
            slots_out, jnp.where(valid, slot_grad, old_slots), current, 0
        )
        passed = shifted(result, "section", -1)
    return (grads_out[None], slots_out[None])


def solution(mesh):
    placed = (
        P("section", None, "expert", None),
        P("section", None, None, None),
        P("section", None, None, None),
        P(None, "expert", None),
        P("section", None, "expert"),
        P("section", None, "expert"),
        P("section", "expert", None),
    )
    return jax.shard_map(
        per_device,
        mesh=mesh,
        in_specs=placed,
        out_specs=(P("section", None, "expert", None), P("section", None, "expert", None)),
        check_vma=False,
    )
```

profile of v0, /device:TPU:0, one launch (start us, length us, event | category | flops | bytes accessed | tf_op | source)
XLA Modules:
  0.0 705.3 jit_solution(5870007492429476042)
XLA Ops:
  6.3 6.5 all-to-all-start
  17.1 16.6 %all-to-all-done = bf16[8,9,3072]{2,1,0:T(8,128)(2,1)S(1)} async-done(((bf16[8,9,3072]{2,1,0:T(8,128)(2,1)}), bf16[8,9,3072]{2,1,0:T(8,128)(2,1)S(1)}, u32[]{:S(2)}, u32[]{:S(2)}) %all-to-all-start) | async-done | bytes 442400 | tf_op jit(solution)/shard_map/all_to_all | solution.py:102
  40.3 18.8 %all-to-all-done.1 = bf16[8,9,3072]{2,1,0:T(8,128)(2,1)S(1)} async-done(((bf16[8,9,3072]{2,1,0:T(8,128)(2,1)}), bf16[8,9,3072]{2,1,0:T(8,128)(2,1)S(1)}, u32[]{:S(2)}, u32[]{:S(2)}) %all-to-all-start.1) | async-done | bytes 442400 | tf_op jit(solution)/shard_map/all_to_all | solution.py:101
  69.2 19.0 %all-to-all-done.2 = bf16[8,9,3072]{2,1,0:T(8,128)(2,1)S(1)} async-done(((bf16[8,9,3072]{2,1,0:T(8,128)(2,1)}), bf16[8,9,3072]{2,1,0:T(8,128)(2,1)S(1)}, u32[]{:S(2)}, u32[]{:S(2)}) %all-to-all-start.2) | async-done | bytes 442400 | tf_op jit(solution)/shard_map/all_to_all | solution.py:118
  95.9 5.7 collective-permute-done
  101.9 11.7 %all-to-all-done.4 = bf16[8,9,3072]{2,1,0:T(8,128)(2,1)S(1)} async-done(((bf16[8,9,3072]{2,1,0:T(8,128)(2,1)}), bf16[8,9,3072]{2,1,0:T(8,128)(2,1)S(1)}, u32[]{:S(2)}, u32[]{:S(2)}) %all-to-all-start.4) | async-done | bytes 442400 | tf_op jit(solution)/shard_map/all_to_all | solution.py:101
  121.8 17.3 %all-to-all-done.3 = bf16[8,9,3072]{2,1,0:T(8,128)(2,1)S(1)} async-done(((bf16[8,9,3072]{2,1,0:T(8,128)(2,1)}), bf16[8,9,3072]{2,1,0:T(8,128)(2,1)S(1)}, u32[]{:S(2)}, u32[]{:S(2)}) %all-to-all-start.3) | async-done | bytes 442400 | tf_op jit(solution)/shard_map/all_to_all | solution.py:102
  147.6 20.0 %all-to-all-done.5 = bf16[8,9,3072]{2,1,0:T(8,128)(2,1)S(1)} async-done(((bf16[8,9,3072]{2,1,0:T(8,128)(2,1)}), bf16[8,9,3072]{2,1,0:T(8,128)(2,1)S(1)}, u32[]{:S(2)}, u32[]{:S(2)}) %all-to-all-start.5) | async-done | bytes 442400 | tf_op jit(solution)/shard_map/all_to_all | solution.py:118
  175.7 5.4 collective-permute-done.1
  181.4 11.7 %all-to-all-done.7 = bf16[8,9,3072]{2,1,0:T(8,128)(2,1)S(1)} async-done(((bf16[8,9,3072]{2,1,0:T(8,128)(2,1)}), bf16[8,9,3072]{2,1,0:T(8,128)(2,1)S(1)}, u32[]{:S(2)}, u32[]{:S(2)}) %all-to-all-start.7) | async-done | bytes 442400 | tf_op jit(solution)/shard_map/all_to_all | solution.py:101
  200.5 17.9 %all-to-all-done.6 = bf16[8,9,3072]{2,1,0:T(8,128)(2,1)S(1)} async-done(((bf16[8,9,3072]{2,1,0:T(8,128)(2,1)}), bf16[8,9,3072]{2,1,0:T(8,128)(2,1)S(1)}, u32[]{:S(2)}, u32[]{:S(2)}) %all-to-all-start.6) | async-done | bytes 442400 | tf_op jit(solution)/shard_map/all_to_all | solution.py:102
  228.6 18.4 %all-to-all-done.8 = bf16[8,9,3072]{2,1,0:T(8,128)(2,1)S(1)} async-done(((bf16[8,9,3072]{2,1,0:T(8,128)(2,1)}), bf16[8,9,3072]{2,1,0:T(8,128)(2,1)S(1)}, u32[]{:S(2)}, u32[]{:S(2)}) %all-to-all-start.8) | async-done | bytes 442400 | tf_op jit(solution)/shard_map/all_to_all | solution.py:118
  255.3 17.0 %all-to-all-done.10 = bf16[8,9,3072]{2,1,0:T(8,128)(2,1)S(1)} async-done(((bf16[8,9,3072]{2,1,0:T(8,128)(2,1)}), bf16[8,9,3072]{2,1,0:T(8,128)(2,1)S(1)}, u32[]{:S(2)}, u32[]{:S(2)}) %all-to-all-start.10) | async-done | bytes 442400 | tf_op jit(solution)/shard_map/all_to_all | solution.py:101
  275.6 141.7 %collective-permute-done.2 = bf16[12,3072]{1,0:T(8,128)(2,1)S(1)} collective-permute-done((bf16[12,3072]{1,0:T(8,128)(2,1)S(1)}, bf16[12,3072]{1,0:T(8,128)(2,1)S(1)}, u32[]{:S(2)}, u32[]{:S(2)}) %collective-permute-start.2) | collective-permute-done | bytes 73760 | tf_op jit(solution)/shard_map/ppermute | solution.py:13
  424.3 19.9 %all-to-all-done.9 = bf16[8,9,3072]{2,1,0:T(8,128)(2,1)S(1)} async-done(((bf16[8,9,3072]{2,1,0:T(8,128)(2,1)}), bf16[8,9,3072]{2,1,0:T(8,128)(2,1)S(1)}, u32[]{:S(2)}, u32[]{:S(2)}) %all-to-all-start.9) | async-done | bytes 442400 | tf_op jit(solution)/shard_map/all_to_all | solution.py:102
  447.4 63.8 %conditional.8 = (bf16[8,9,3072]{2,1,0:T(8,128)(2,1)}, bf16[8,9]{1,0:T(8,128)(2,1)}) conditional(s32[]{:T(128)} %convert_element_type.358, () %tuple.54, (f32[8,9]{1,0:T(8,128)S(1)}, bf16[8,9,3072]{2,1,0:T(8,128)(2,1)S(1)}, bf16[4096,3072]{1,0:T(8,128)(2,1)}, bf16[8,9,3072]{2,1,0:T(8,128)(2,1)S(1)}, bf16[3072,4096]{1,0:T(8,128)(2,1)}, ...), branch_computations={%region_24.25_spmd, %region_25.27_spmd} | conditional | flops 9067511808 | bytes 147359952 | solution.py:114
  448.2 10.6 %fusion.139 = f32[72,4096]{1,0:T(8,128)S(1)} fusion(bf16[72,3072]{1,0:T(8,128)(2,1)S(1)} %reshape.293, bf16[3072,4096]{1,0:T(8,128)(2,1)} %get-tuple-element.83), kind=kOutput, calls=%fused_computation.273 | convolution fusion | flops 1811939328 | bytes 26787840 | tf_op jit(solution)/shard_map/cond/branch_1_fun/dot_general | solution.py:35
  459.1 12.5 %fusion.138 = f32[72,4096]{1,0:T(8,128)S(1)} fusion(bf16[72,3072]{1,0:T(8,128)(2,1)S(1)} %reshape.292, bf16[4096,3072]{1,0:T(8,128)(2,1)} %get-tuple-element.80), kind=kOutput, calls=%fused_computation.272 | convolution fusion | flops 1811939328 | bytes 26787840 | tf_op jit(solution)/shard_map/cond/branch_1_fun/rd,fd->rf/dot_general | solution.py:37
  471.6 11.2 %multiply_reduce_fusion.3 = (bf16[72]{0:T(256)(128)(2,1)}, f32[72,4096]{1,0:T(8,128)S(1)}) fusion(f32[72,4096]{1,0:T(8,128)S(1)} %fusion.138, f32[72,4096]{1,0:T(8,128)S(1)} %fusion.139, bf16[72,3072]{1,0:T(8,128)(2,1)S(1)} %copy-done.7, bf16[3072,4096]{1,0:T(8,128)(2,1)} %get-tuple-element.82), kind=kOutput, calls=%fused_computation.37 | convolution fusion | flops 1814003584 | bytes 29147280 | tf_op jit(solution)/shard_map/cond/branch_1_fun/dot_general | solution.py:36
  482.9 13.5 %fusion.25 = f32[72,3072]{1,0:T(8,128)} fusion(bf16[3072,4096]{1,0:T(8,128)(2,1)} %get-tuple-element.83, f32[72,4096]{1,0:T(8,128)S(1)} %fusion.139, f32[72,4096]{1,0:T(8,128)S(1)} %get-tuple-element.133, f32[72,4096]{1,0:T(8,128)S(1)} %fusion.138, f32[72]{0:T(128)S(1)} %mul.208), kind=kOutput, calls=%fused_computation.42 | convolution fusion | flops 1815183360 | bytes 29589792 | tf_op jit(solution)/shard_map/cond/branch_1_fun/rf,df->rd/dot_general | solution.py:43
  496.4 12.9 %convolution_add_fusion.3 = bf16[72,3072]{1,0:T(8,128)(2,1)S(1)} fusion(f32[72,3072]{1,0:T(8,128)} %fusion.25, bf16[3072,4096]{1,0:T(8,128)(2,1)} %get-tuple-element.82, f32[72,4096]{1,0:T(8,128)S(1)} %fusion.138, f32[72]{0:T(128)S(1)} %mul.208, f32[72,4096]{1,0:T(8,128)S(1)} %fusion.139), kind=kOutput, calls=%fused_computation.36 | convolution fusion | flops 1814446080 | bytes 28852512 | tf_op jit(solution)/shard_map/cond/branch_1_fun/rf,df->rd/dot_general | solution.py:44
  511.3 5.1 all-to-all-start.11
  518.5 18.9 %all-to-all-done.11 = bf16[8,9,3072]{2,1,0:T(8,128)(2,1)S(1)} async-done(((bf16[8,9,3072]{2,1,0:T(8,128)(2,1)}), bf16[8,9,3072]{2,1,0:T(8,128)(2,1)S(1)}, u32[]{:S(2)}, u32[]{:S(2)}) %all-to-all-start.11) | async-done | bytes 442400 | tf_op jit(solution)/shard_map/all_to_all | solution.py:118
  545.2 17.6 %all-to-all-done.13 = bf16[8,9,3072]{2,1,0:T(8,128)(2,1)S(1)} async-done(((bf16[8,9,3072]{2,1,0:T(8,128)(2,1)}), bf16[8,9,3072]{2,1,0:T(8,128)(2,1)S(1)}, u32[]{:S(2)}, u32[]{:S(2)}) %all-to-all-start.13) | async-done | bytes 442400 | tf_op jit(solution)/shard_map/all_to_all | solution.py:101
  586.0 19.8 %all-to-all-done.12 = bf16[8,9,3072]{2,1,0:T(8,128)(2,1)S(1)} async-done(((bf16[8,9,3072]{2,1,0:T(8,128)(2,1)}), bf16[8,9,3072]{2,1,0:T(8,128)(2,1)S(1)}, u32[]{:S(2)}, u32[]{:S(2)}) %all-to-all-start.12) | async-done | bytes 442400 | tf_op jit(solution)/shard_map/all_to_all | solution.py:102
  605.8 63.3 %conditional.9 = (bf16[8,9,3072]{2,1,0:T(8,128)(2,1)}, bf16[8,9]{1,0:T(8,128)(2,1)S(1)}) conditional(s32[]{:T(128)} %convert_element_type.369, () %tuple.56, (f32[8,9]{1,0:T(8,128)S(1)}, bf16[8,9,3072]{2,1,0:T(8,128)(2,1)S(1)}, bf16[4096,3072]{1,0:T(8,128)(2,1)}, bf16[8,9,3072]{2,1,0:T(8,128)(2,1)S(1)}, bf16[3072,4096]{1,0:T(8,128)(2,1)}, ...), branch_computations={%region_31.32_spmd, %region_32.34_spmd} | conditional | flops 9067511808 | bytes 147359952 | solution.py:114
  606.2 10.6 %fusion.141 = f32[72,4096]{1,0:T(8,128)S(1)} fusion(bf16[72,3072]{1,0:T(8,128)(2,1)S(1)} %reshape.297, bf16[3072,4096]{1,0:T(8,128)(2,1)} %get-tuple-element.89), kind=kOutput, calls=%fused_computation.275 | convolution fusion | flops 1811939328 | bytes 26787840 | tf_op jit(solution)/shard_map/cond/branch_1_fun/dot_general | solution.py:35
  617.1 12.5 %fusion.140 = f32[72,4096]{1,0:T(8,128)S(1)} fusion(bf16[72,3072]{1,0:T(8,128)(2,1)S(1)} %reshape.296, bf16[4096,3072]{1,0:T(8,128)(2,1)} %get-tuple-element.86), kind=kOutput, calls=%fused_computation.274 | convolution fusion | flops 1811939328 | bytes 26787840 | tf_op jit(solution)/shard_map/cond/branch_1_fun/rd,fd->rf/dot_general | solution.py:37
  629.7 11.3 %multiply_reduce_fusion.4 = (bf16[72]{0:T(256)(128)(2,1)}, f32[72,4096]{1,0:T(8,128)S(1)}) fusion(f32[72,4096]{1,0:T(8,128)S(1)} %fusion.140, f32[72,4096]{1,0:T(8,128)S(1)} %fusion.141, bf16[72,3072]{1,0:T(8,128)(2,1)S(1)} %copy-done.9, bf16[3072,4096]{1,0:T(8,128)(2,1)} %get-tuple-element.88), kind=kOutput, calls=%fused_computation.49 | convolution fusion | flops 1814003584 | bytes 29147280 | tf_op jit(solution)/shard_map/cond/branch_1_fun/dot_general | solution.py:36
  641.0 13.5 %fusion.33 = f32[72,3072]{1,0:T(8,128)} fusion(bf16[3072,4096]{1,0:T(8,128)(2,1)} %get-tuple-element.89, f32[72,4096]{1,0:T(8,128)S(1)} %fusion.141, f32[72,4096]{1,0:T(8,128)S(1)} %get-tuple-element.135, f32[72,4096]{1,0:T(8,128)S(1)} %fusion.140, f32[72]{0:T(128)S(1)} %mul.219), kind=kOutput, calls=%fused_computation.54 | convolution fusion | flops 1815183360 | bytes 29589792 | tf_op jit(solution)/shard_map/cond/branch_1_fun/rf,df->rd/dot_general | solution.py:43
  654.6 13.0 %convolution_add_fusion.4 = bf16[72,3072]{1,0:T(8,128)(2,1)S(1)} fusion(f32[72,3072]{1,0:T(8,128)} %fusion.33, bf16[3072,4096]{1,0:T(8,128)(2,1)} %get-tuple-element.88, f32[72,4096]{1,0:T(8,128)S(1)} %fusion.140, f32[72]{0:T(128)S(1)} %mul.219, f32[72,4096]{1,0:T(8,128)S(1)} %fusion.141), kind=kOutput, calls=%fused_computation.48 | convolution fusion | flops 1814446080 | bytes 28852512 | tf_op jit(solution)/shard_map/cond/branch_1_fun/rf,df->rd/dot_general | solution.py:44
  682.7 20.3 %all-to-all-done.14 = bf16[8,9,3072]{2,1,0:T(8,128)(2,1)S(1)} async-done(((bf16[8,9,3072]{2,1,0:T(8,128)(2,1)}), bf16[8,9,3072]{2,1,0:T(8,128)(2,1)S(1)}, u32[]{:S(2)}, u32[]{:S(2)}) %all-to-all-start.14) | async-done | bytes 442400 | tf_op jit(solution)/shard_map/all_to_all | solution.py:118
  (348 shorter events, 153.1 us)
Async XLA Ops:
  6.3 27.4 %all-to-all-start = ((bf16[8,9,3072]{2,1,0:T(8,128)(2,1)}), bf16[8,9,3072]{2,1,0:T(8,128)(2,1)S(1)}, u32[]{:S(2)}, u32[]{:S(2)}) async-start(bf16[8,9,3072]{2,1,0:T(8,128)(2,1)} %bitcast.16), calls=%async_computation | async-start | bytes 1572864 | tf_op jit(solution)/shard_map/all_to_all | solution.py:102
  34.7 24.4 %all-to-all-start.1 = ((bf16[8,9,3072]{2,1,0:T(8,128)(2,1)}), bf16[8,9,3072]{2,1,0:T(8,128)(2,1)S(1)}, u32[]{:S(2)}, u32[]{:S(2)}) async-start(bf16[8,9,3072]{2,1,0:T(8,128)(2,1)} %bitcast.20), calls=%async_computation.1 | async-start | bytes 1572864 | tf_op jit(solution)/shard_map/all_to_all | solution.py:101
  63.6 24.6 %all-to-all-start.2 = ((bf16[8,9,3072]{2,1,0:T(8,128)(2,1)}), bf16[8,9,3072]{2,1,0:T(8,128)(2,1)S(1)}, u32[]{:S(2)}, u32[]{:S(2)}) async-start(bf16[8,9,3072]{2,1,0:T(8,128)(2,1)} %get-tuple-element.102), calls=%async_computation.2 | async-start | bytes 1572864 | tf_op jit(solution)/shard_map/all_to_all | solution.py:118
  68.3 50.2 %copy-start.32 = (f32[1,4,9,24]{2,3,1,0:T(8,128)}, f32[1,4,9,24]{2,3,1,0:T(8,128)S(1)}, u32[]{:S(2)}) copy-start(f32[1,4,9,24]{2,3,1,0:T(8,128)S(1)} %get-tuple-element.160) | copy-start | bytes 10372
  89.2 24.4 %all-to-all-start.4 = ((bf16[8,9,3072]{2,1,0:T(8,128)(2,1)}), bf16[8,9,3072]{2,1,0:T(8,128)(2,1)S(1)}, u32[]{:S(2)}, u32[]{:S(2)}) async-start(bf16[8,9,3072]{2,1,0:T(8,128)(2,1)} %bitcast.35), calls=%async_computation.4 | async-start | bytes 1572864 | tf_op jit(solution)/shard_map/all_to_all | solution.py:101
  94.6 7.0 collective-permute-start
  114.6 24.6 %all-to-all-start.3 = ((bf16[8,9,3072]{2,1,0:T(8,128)(2,1)}), bf16[8,9,3072]{2,1,0:T(8,128)(2,1)S(1)}, u32[]{:S(2)}, u32[]{:S(2)}) async-start(bf16[8,9,3072]{2,1,0:T(8,128)(2,1)} %bitcast.32), calls=%async_computation.3 | async-start | bytes 1572864 | tf_op jit(solution)/shard_map/all_to_all | solution.py:102
  143.0 25.6 %copy-start.70 = (bf16[8,9]{1,0:T(8,128)(2,1)}, bf16[8,9]{1,0:T(8,128)(2,1)S(1)}, u32[]{:S(2)}) copy-start(bf16[8,9]{1,0:T(8,128)(2,1)S(1)} %get-tuple-element.108) | copy-start | bytes 436
  143.1 24.6 %all-to-all-start.5 = ((bf16[8,9,3072]{2,1,0:T(8,128)(2,1)}), bf16[8,9,3072]{2,1,0:T(8,128)(2,1)S(1)}, u32[]{:S(2)}, u32[]{:S(2)}) async-start(bf16[8,9,3072]{2,1,0:T(8,128)(2,1)} %get-tuple-element.103), calls=%async_computation.5 | async-start | bytes 1572864 | tf_op jit(solution)/shard_map/all_to_all | solution.py:118
  168.6 24.4 %all-to-all-start.7 = ((bf16[8,9,3072]{2,1,0:T(8,128)(2,1)}), bf16[8,9,3072]{2,1,0:T(8,128)(2,1)S(1)}, u32[]{:S(2)}, u32[]{:S(2)}) async-start(bf16[8,9,3072]{2,1,0:T(8,128)(2,1)} %bitcast.49), calls=%async_computation.7 | async-start | bytes 1572864 | tf_op jit(solution)/shard_map/all_to_all | solution.py:101
  174.1 7.0 collective-permute-start.1
  194.0 24.4 %all-to-all-start.6 = ((bf16[8,9,3072]{2,1,0:T(8,128)(2,1)}), bf16[8,9,3072]{2,1,0:T(8,128)(2,1)S(1)}, u32[]{:S(2)}, u32[]{:S(2)}) async-start(bf16[8,9,3072]{2,1,0:T(8,128)(2,1)} %bitcast.46), calls=%async_computation.6 | async-start | bytes 1572864 | tf_op jit(solution)/shard_map/all_to_all | solution.py:102
  222.4 24.6 %all-to-all-start.8 = ((bf16[8,9,3072]{2,1,0:T(8,128)(2,1)}), bf16[8,9,3072]{2,1,0:T(8,128)(2,1)S(1)}, u32[]{:S(2)}, u32[]{:S(2)}) async-start(bf16[8,9,3072]{2,1,0:T(8,128)(2,1)} %get-tuple-element.104), calls=%async_computation.8 | async-start | bytes 1572864 | tf_op jit(solution)/shard_map/all_to_all | solution.py:118
  247.9 24.4 %all-to-all-start.10 = ((bf16[8,9,3072]{2,1,0:T(8,128)(2,1)}), bf16[8,9,3072]{2,1,0:T(8,128)(2,1)S(1)}, u32[]{:S(2)}, u32[]{:S(2)}) async-start(bf16[8,9,3072]{2,1,0:T(8,128)(2,1)} %bitcast.63), calls=%async_computation.10 | async-start | bytes 1572864 | tf_op jit(solution)/shard_map/all_to_all | solution.py:101
  251.6 165.7 %copy-start.24 = (bf16[1,12,3072]{2,0,1:T(2,128)(2,1)S(1)}, bf16[1,12,3072]{2,0,1:T(2,128)(2,1)}, u32[]{:S(2)}) copy-start(bf16[1,12,3072]{2,0,1:T(2,128)(2,1)} %get-tuple-element.142) | copy-start | bytes 221188
  253.4 165.1 %copy-start.16 = (bf16[2,12,3072]{2,1,0:T(8,128)(2,1)}, bf16[2,12,3072]{2,1,0:T(8,128)(2,1)S(1)}, u32[]{:S(2)}) copy-start(bf16[2,12,3072]{2,1,0:T(8,128)(2,1)S(1)} %get-tuple-element.122) | copy-start | bytes 442372
  253.4 163.8 %collective-permute-start.2 = (bf16[12,3072]{1,0:T(8,128)(2,1)S(1)}, bf16[12,3072]{1,0:T(8,128)(2,1)S(1)}, u32[]{:S(2)}, u32[]{:S(2)}) collective-permute-start(bf16[12,3072]{1,0:T(8,128)(2,1)S(1)} %get-tuple-element.123), channel_id=1, source_target_pairs={{8,0},{16,8},{24,16},{9,1},{17,9},{25,17},{10,2},{18,10},{26,18},{... | collective-permute-start | bytes 221192 | tf_op jit(solution)/shard_map/ppermute | solution.py:13
  272.4 145.2 %all-to-all-start.15 = ((bf16[8,1,9]{2,1,0:T(2,128)(2,1)}), bf16[8,1,9]{2,1,0:T(2,128)(2,1)S(1)}, u32[]{:S(2)}, u32[]{:S(2)}) async-start(bf16[8,1,9]{2,1,0:T(2,128)(2,1)} %copy.218), calls=%async_computation.15 | async-start | bytes 8192 | tf_op jit(solution)/shard_map/all_to_all | solution.py:119
  418.5 25.7 %all-to-all-start.9 = ((bf16[8,9,3072]{2,1,0:T(8,128)(2,1)}), bf16[8,9,3072]{2,1,0:T(8,128)(2,1)S(1)}, u32[]{:S(2)}, u32[]{:S(2)}) async-start(bf16[8,9,3072]{2,1,0:T(8,128)(2,1)} %bitcast.60), calls=%async_computation.9 | async-start | bytes 1572864 | tf_op jit(solution)/shard_map/all_to_all | solution.py:102
  444.2 67.1 %all-to-all-start.16 = ((bf16[8,1,9]{2,1,0:T(2,128)(2,1)}), bf16[8,1,9]{2,1,0:T(2,128)(2,1)S(1)}, u32[]{:S(2)}, u32[]{:S(2)}) async-start(bf16[8,1,9]{2,1,0:T(2,128)(2,1)} %copy.220), calls=%async_computation.16 | async-start | bytes 8192 | tf_op jit(solution)/shard_map/all_to_all | solution.py:119
  511.3 26.1 %all-to-all-start.11 = ((bf16[8,9,3072]{2,1,0:T(8,128)(2,1)}), bf16[8,9,3072]{2,1,0:T(8,128)(2,1)S(1)}, u32[]{:S(2)}, u32[]{:S(2)}) async-start(bf16[8,9,3072]{2,1,0:T(8,128)(2,1)} %get-tuple-element.105), calls=%async_computation.11 | async-start | bytes 1572864 | tf_op jit(solution)/shard_map/all_to_all | solution.py:118
  518.5 23.5 %copy-start.73 = (bf16[8,9]{1,0:T(8,128)(2,1)S(1)}, bf16[8,9]{1,0:T(8,128)(2,1)}, u32[]{:S(2)}) copy-start(bf16[8,9]{1,0:T(8,128)(2,1)} %copy-done.72) | copy-start | bytes 436
  518.5 24.1 %copy-start.17 = (bf16[2,12,3072]{2,1,0:T(8,128)(2,1)S(1)}, bf16[2,12,3072]{2,1,0:T(8,128)(2,1)}, u32[]{:S(2)}) copy-start(bf16[2,12,3072]{2,1,0:T(8,128)(2,1)} %copy-done.16) | copy-start | bytes 442372
  538.4 24.4 %all-to-all-start.13 = ((bf16[8,9,3072]{2,1,0:T(8,128)(2,1)}), bf16[8,9,3072]{2,1,0:T(8,128)(2,1)S(1)}, u32[]{:S(2)}, u32[]{:S(2)}) async-start(bf16[8,9,3072]{2,1,0:T(8,128)(2,1)} %bitcast.78), calls=%async_computation.13 | async-start | bytes 1572864 | tf_op jit(solution)/shard_map/all_to_all | solution.py:101
  542.6 32.9 %copy-start.22 = (bf16[1,12,3072]{2,0,1:T(2,128)(2,1)S(1)}, bf16[1,12,3072]{2,0,1:T(2,128)(2,1)}, u32[]{:S(2)}) copy-start(bf16[1,12,3072]{2,0,1:T(2,128)(2,1)} %get-tuple-element.141) | copy-start | bytes 221188
  543.9 37.5 %copy-start.18 = (bf16[2,12,3072]{2,1,0:T(8,128)(2,1)}, bf16[2,12,3072]{2,1,0:T(8,128)(2,1)S(1)}, u32[]{:S(2)}) copy-start(bf16[2,12,3072]{2,1,0:T(8,128)(2,1)S(1)} %get-tuple-element.120) | copy-start | bytes 442372
  543.9 31.0 %collective-permute-start.3 = (bf16[12,3072]{1,0:T(8,128)(2,1)S(1)}, bf16[12,3072]{1,0:T(8,128)(2,1)S(1)}, u32[]{:S(2)}, u32[]{:S(2)}) collective-permute-start(bf16[12,3072]{1,0:T(8,128)(2,1)S(1)} %get-tuple-element.121), channel_id=1, source_target_pairs={{8,0},{16,8},{24,16},{9,1},{17,9},{25,17},{10,2},{18,10},{26,18},{... | collective-permute-start | bytes 221192 | tf_op jit(solution)/shard_map/ppermute | solution.py:13
  562.8 8.7 %all-to-all-start.17 = ((bf16[8,1,9]{2,1,0:T(2,128)(2,1)}), bf16[8,1,9]{2,1,0:T(2,128)(2,1)S(1)}, u32[]{:S(2)}, u32[]{:S(2)}) async-start(bf16[8,1,9]{2,1,0:T(2,128)(2,1)} %copy.222), calls=%async_computation.17 | async-start | bytes 8192 | tf_op jit(solution)/shard_map/all_to_all | solution.py:119
  571.5 8.9 %all-to-all-start.18 = ((bf16[8,1,9]{2,1,0:T(2,128)(2,1)}), bf16[8,1,9]{2,1,0:T(2,128)(2,1)S(1)}, u32[]{:S(2)}, u32[]{:S(2)}) async-start(bf16[8,1,9]{2,1,0:T(2,128)(2,1)} %copy.224), calls=%async_computation.18 | async-start | bytes 8192 | tf_op jit(solution)/shard_map/all_to_all | solution.py:119
  581.4 24.4 %all-to-all-start.12 = ((bf16[8,9,3072]{2,1,0:T(8,128)(2,1)}), bf16[8,9,3072]{2,1,0:T(8,128)(2,1)S(1)}, u32[]{:S(2)}, u32[]{:S(2)}) async-start(bf16[8,9,3072]{2,1,0:T(8,128)(2,1)} %bitcast.75), calls=%async_computation.12 | async-start | bytes 1572864 | tf_op jit(solution)/shard_map/all_to_all | solution.py:102
  669.7 8.9 %all-to-all-start.19 = ((bf16[8,1,9]{2,1,0:T(2,128)(2,1)}), bf16[8,1,9]{2,1,0:T(2,128)(2,1)S(1)}, u32[]{:S(2)}, u32[]{:S(2)}) async-start(bf16[8,1,9]{2,1,0:T(2,128)(2,1)} %copy.226), calls=%async_computation.19 | async-start | bytes 8192 | tf_op jit(solution)/shard_map/all_to_all | solution.py:119
  678.6 24.4 %all-to-all-start.14 = ((bf16[8,9,3072]{2,1,0:T(8,128)(2,1)}), bf16[8,9,3072]{2,1,0:T(8,128)(2,1)S(1)}, u32[]{:S(2)}, u32[]{:S(2)}) async-start(bf16[8,9,3072]{2,1,0:T(8,128)(2,1)} %get-tuple-element.106), calls=%async_computation.14 | async-start | bytes 1572864 | tf_op jit(solution)/shard_map/all_to_all | solution.py:118
  (70 other events, 557.9 us)
where the time goes:
time: 711 us; the launch traced here: 705 us
  waiting for transfers between devices  431 us (61%)
  matrix products  132 us (19%)
  starting transfers between devices  81 us (11%)
  local copies, waits for them, and re-layouts  37.3 us (5%)
  loops' own time  10.9 us (2%)
  other arithmetic  10.1 us (1%)
    ppermute x4, waiting for transfers between devices, shifted(): return lax.ppermute(shard, axis, pairs)  153 us
    all_to_all x5, waiting for transfers between devices, per_device(): lax.all_to_all(moved_half, 'expert', split_axis=0, concat_axis=0, tiled=T...  96.6 us
    all_to_all x5, waiting for transfers between devices, per_device(): lax.all_to_all(sent_grads, 'expert', split_axis=0, concat_axis=0, tiled=T...  91.5 us
    all_to_all x5, waiting for transfers between devices, per_device(): lax.all_to_all(sent_inputs, 'expert', split_axis=0, concat_axis=0, tiled=...  76.9 us
    dot_general x2, matrix products, expert_grads(): jnp.einsum('rf,df->rd', gate_grad, gate_part, preferred_element_type=jnp....  27.1 us
    dot_general x2, matrix products, expert_grads(): jnp.einsum('rf,df->rd', lift_grad, lift_part, preferred_element_type=jnp....  25.9 us
    dot_general x2, matrix products, expert_grads(): jnp.einsum('rd,fd->rf', grads, down_part, preferred_element_type=jnp.floa...  25.1 us
    dot_general x2, matrix products, expert_grads(): pre_lift = jnp.dot(inputs, lift_part, preferred_element_type=jnp.float32)  22.5 us
  transfers between devices with their start and end apart: 24, of which 21 were waited for; matrix products, arithmetic and copies ran while one was open for 13% of the time, Pallas kernels for 0%

commit v1 on v0

--- a/solution.py
+++ b/solution.py
@@ -5,6 +5,28 @@
 
 EXPERTS = 4
 CAP = 9
+
+
+def step_on_bands(frame, row_axis):
+    v_next = lax.psum(1, row_axis)
+    far_arr, tall = (v_next, lax.axis_index(row_axis))
+    s_next = frame.shape[0] // far_arr
+    then = list(frame.shape)
+    then[0] = s_next
+    n_now = then[0]
+    then[0] = n_now * far_arr
+    right_arr = jnp.zeros(then, frame.dtype)
+    rr = 0
+    while rr < far_arr:
+        part_next = lax.dynamic_slice_in_dim(frame, (tall ^ rr) * s_next, s_next, axis=0)
+        if rr:
+            row_out = tuple(((ix, ix ^ rr) for ix in range(far_arr)))
+            part_next = lax.ppermute(part_next, row_axis, row_out)
+        right_arr = lax.dynamic_update_slice_in_dim(
+            right_arr, part_next, (tall ^ rr) * n_now, axis=0
+        )
+        rr += 1
+    return right_arr
 
 
 def shifted(shard, axis, by):
@@ -99,7 +121,7 @@
         sent_grads = jnp.repeat(sent_grads, group, axis=0)
         got_inputs, got_grads = (
             lax.all_to_all(sent_inputs, "expert", split_axis=0, concat_axis=0, tiled=True),
-            lax.all_to_all(sent_grads, "expert", split_axis=0, concat_axis=0, tiled=True),
+            step_on_bands(sent_grads, "expert"),
         )
 
         def active_case(first, second):

time: 711 us -> 683 us (0.961)
  waiting for transfers between devices: 431 us -> 355 us
  starting transfers between devices: 81 us -> 116 us
    all_to_all x5 -> x0, waiting for transfers between devices: 91.5 us -> none  [per_device(): lax.all_to_all(sent_grads, 'expert', split_axis=0, concat_axis=0, tiled=T...]
    all_to_all x5, waiting for transfers between devices: 76.9 us -> 4.32 us  [per_device(): lax.all_to_all(sent_inputs, 'expert', split_axis=0, concat_axis=0, tiled=...]
    ppermute x4, waiting for transfers between devices: 153 us -> 201 us  [shifted(): return lax.ppermute(shard, axis, pairs)]
    ppermute x0 -> x35, waiting for transfers between devices: none -> 45.5 us  [step_on_bands(): part_next = lax.ppermute(part_next, row_axis, row_out)]
    ppermute x0 -> x35, starting transfers between devices: none -> 43.5 us  [step_on_bands(): part_next = lax.ppermute(part_next, row_axis, row_out)]
    all_to_all x5 -> x0, starting transfers between devices: 22 us -> none  [per_device(): lax.all_to_all(sent_grads, 'expert', split_axis=0, concat_axis=0, tiled=T...]
  transfers between devices with their start and end apart: 24 -> 54, of which waited for: 21 -> 24; matrix products, arithmetic and copies ran while one was open for 13% -> 16% of each run, Pallas kernels for 0% -> 0%
where the time goes in v1:
time: 683 us; the launch traced here: 676 us
  waiting for transfers between devices  355 us (52%)
  matrix products  137 us (20%)
  starting transfers between devices  116 us (17%)
  local copies, waits for them, and re-layouts  42.6 us (6%)
  loops' own time  11.7 us (2%)
  other arithmetic  10.8 us (2%)
    ppermute x4, waiting for transfers between devices, shifted(): return lax.ppermute(shard, axis, pairs)  201 us
    all_to_all x5, waiting for transfers between devices, per_device(): lax.all_to_all(moved_half, 'expert', split_axis=0, concat_axis=0, tiled=T...  92.6 us
    ppermute x35, waiting for transfers between devices, step_on_bands(): part_next = lax.ppermute(part_next, row_axis, row_out)  45.5 us
    ppermute x35, starting transfers between devices, step_on_bands(): part_next = lax.ppermute(part_next, row_axis, row_out)  43.5 us
    dot_general x2, matrix products, expert_grads(): jnp.einsum('rf,df->rd', gate_grad, gate_part, preferred_element_type=jnp....  27.1 us
    all_to_all x5, starting transfers between devices, per_device(): lax.all_to_all(moved_half, 'expert', split_axis=0, concat_axis=0, tiled=T...  26.1 us
    dot_general x2, matrix products, expert_grads(): jnp.einsum('rf,df->rd', lift_grad, lift_part, preferred_element_type=jnp....  26 us
    dot_general x2, matrix products, expert_grads(): jnp.einsum('rd,fd->rf', grads, down_part, preferred_element_type=jnp.floa...  25.1 us
  transfers between devices with their start and end apart: 54, of which 24 were waited for; matrix products, arithmetic and copies ran while one was open for 16% of the time, Pallas kernels for 0%

profile of v1, /device:TPU:0, one launch (start us, length us, event | category | flops | bytes accessed | tf_op | source)
XLA Modules:
  0.0 676.3 jit_solution(14403043887169482954)
XLA Ops:
  14.4 4.9 all-to-all-start
  31.7 8.2 %collective-permute-done.5 = bf16[1,9,3072]{2,1,0:T(8,128)(2,1)S(1)} collective-permute-done((bf16[1,9,3072]{2,1,0:T(8,128)(2,1)S(1)}, bf16[1,9,3072]{2,1,0:T(8,128)(2,1)S(1)}, u32[]{:S(2)}, u32[]{:S(2)}) %collective-permute-start.5) | collective-permute-done | bytes 55328 | tf_op jit(solution)/shard_map/ppermute | solution.py:24
  45.1 5.0 conditional.5
  50.1 5.6 all-to-all-start.1
  59.2 17.5 %all-to-all-done.1 = bf16[8,9,3072]{2,1,0:T(8,128)(2,1)S(1)} async-done(((bf16[8,9,3072]{2,1,0:T(8,128)(2,1)}), bf16[8,9,3072]{2,1,0:T(8,128)(2,1)S(1)}, u32[]{:S(2)}, u32[]{:S(2)}) %all-to-all-start.1) | async-done | bytes 442400 | tf_op jit(solution)/shard_map/all_to_all | solution.py:140
  85.1 5.0 collective-permute-done.7
  99.4 13.7 %collective-permute-done.11 = bf16[1,9,3072]{2,1,0:T(8,128)(2,1)S(1)} collective-permute-done((bf16[1,9,3072]{2,1,0:T(8,128)(2,1)S(1)}, bf16[1,9,3072]{2,1,0:T(8,128)(2,1)S(1)}, u32[]{:S(2)}, u32[]{:S(2)}) %collective-permute-start.11) | collective-permute-done | bytes 55328 | tf_op jit(solution)/shard_map/ppermute | solution.py:24
  117.7 5.0 conditional.6
  128.2 19.1 %all-to-all-done.3 = bf16[8,9,3072]{2,1,0:T(8,128)(2,1)S(1)} async-done(((bf16[8,9,3072]{2,1,0:T(8,128)(2,1)}), bf16[8,9,3072]{2,1,0:T(8,128)(2,1)S(1)}, u32[]{:S(2)}, u32[]{:S(2)}) %all-to-all-start.3) | async-done | bytes 442400 | tf_op jit(solution)/shard_map/all_to_all | solution.py:140
  174.5 4.7 all-to-all-start.10
  189.7 6.1 all-to-all-start.5
  199.8 17.0 %all-to-all-done.5 = bf16[8,9,3072]{2,1,0:T(8,128)(2,1)S(1)} async-done(((bf16[8,9,3072]{2,1,0:T(8,128)(2,1)}), bf16[8,9,3072]{2,1,0:T(8,128)(2,1)S(1)}, u32[]{:S(2)}, u32[]{:S(2)}) %all-to-all-start.5) | async-done | bytes 442400 | tf_op jit(solution)/shard_map/all_to_all | solution.py:140
  230.1 179.4 %collective-permute-done.23 = bf16[12,3072]{1,0:T(8,128)(2,1)S(1)} collective-permute-done((bf16[12,3072]{1,0:T(8,128)(2,1)S(1)}, bf16[12,3072]{1,0:T(8,128)(2,1)S(1)}, u32[]{:S(2)}, u32[]{:S(2)}) %collective-permute-start.23) | collective-permute-done | bytes 73760 | tf_op jit(solution)/shard_map/ppermute | solution.py:35
  429.0 67.3 %conditional.8 = (bf16[8,9,3072]{2,1,0:T(8,128)(2,1)}, bf16[8,9]{1,0:T(8,128)(2,1)}) conditional(s32[]{:T(128)} %convert_element_type.378, () %tuple.74, (f32[8,9]{1,0:T(8,128)}, bf16[8,9,3072]{2,1,0:T(8,128)(2,1)S(1)}, s32[]{:T(128)}, bf16[1,9,3072]{2,1,0:T(8,128)(2,1)S(1)}, s32[]{:T(128)}, /*index=5*/bf16[1,9,3072]{2,1,0:T(8,128)(2,1)S(1)}, ...), branch_computations={%region_24.25_spmd, %region_25.27_spmd} | conditional | flops 9067511808 | bytes 151144912 | solution.py:136
  430.1 10.6 %fusion.139 = f32[72,4096]{1,0:T(8,128)S(1)} fusion(bf16[72,3072]{1,0:T(8,128)(2,1)S(1)} %reshape.333, bf16[3072,4096]{1,0:T(8,128)(2,1)} %get-tuple-element.893), kind=kOutput, calls=%fused_computation.348 | convolution fusion | flops 1811939328 | bytes 26787840 | tf_op jit(solution)/shard_map/cond/branch_1_fun/dot_general | solution.py:57
  442.8 12.5 %fusion.138 = f32[72,4096]{1,0:T(8,128)S(1)} fusion(bf16[72,3072]{1,0:T(8,128)(2,1)} %reshape.332, bf16[4096,3072]{1,0:T(8,128)(2,1)} %get-tuple-element.890), kind=kOutput, calls=%fused_computation.347 | convolution fusion | flops 1811939328 | bytes 26787840 | tf_op jit(solution)/shard_map/cond/branch_1_fun/rd,fd->rf/dot_general | solution.py:59
  455.3 11.2 %multiply_reduce_fusion.3 = (bf16[72]{0:T(256)(128)(2,1)}, f32[72,4096]{1,0:T(8,128)S(1)}) fusion(f32[72,4096]{1,0:T(8,128)S(1)} %fusion.138, f32[72,4096]{1,0:T(8,128)S(1)} %fusion.139, bf16[72,3072]{1,0:T(8,128)(2,1)S(1)} %copy-done.7, bf16[3072,4096]{1,0:T(8,128)(2,1)} %get-tuple-element.892), kind=kOutput, calls=%fused_computation.61 | convolution fusion | flops 1814003584 | bytes 29147280 | tf_op jit(solution)/shard_map/cond/branch_1_fun/dot_general | solution.py:58
  467.9 13.5 %fusion.25 = f32[72,3072]{1,0:T(8,128)} fusion(bf16[3072,4096]{1,0:T(8,128)(2,1)} %get-tuple-element.893, f32[72,4096]{1,0:T(8,128)S(1)} %fusion.139, f32[72,4096]{1,0:T(8,128)S(1)} %get-tuple-element.958, f32[72,4096]{1,0:T(8,128)S(1)} %fusion.138, f32[72]{0:T(128)} %mul.318), kind=kOutput, calls=%fused_computation.66 | convolution fusion | flops 1815183360 | bytes 29589792 | tf_op jit(solution)/shard_map/cond/branch_1_fun/rf,df->rd/dot_general | solution.py:65
  481.4 12.9 %convolution_add_fusion.3 = bf16[72,3072]{1,0:T(8,128)(2,1)S(1)} fusion(f32[72,3072]{1,0:T(8,128)} %fusion.25, bf16[3072,4096]{1,0:T(8,128)(2,1)} %get-tuple-element.892, f32[72,4096]{1,0:T(8,128)S(1)} %fusion.138, f32[72]{0:T(128)} %mul.318, f32[72,4096]{1,0:T(8,128)S(1)} %fusion.139), kind=kOutput, calls=%fused_computation.60 | convolution fusion | flops 1814446080 | bytes 28852512 | tf_op jit(solution)/shard_map/cond/branch_1_fun/rf,df->rd/dot_general | solution.py:66
  496.4 7.3 %all-to-all-start.7 = ((bf16[8,9,3072]{2,1,0:T(8,128)(2,1)}), bf16[8,9,3072]{2,1,0:T(8,128)(2,1)S(1)}, u32[]{:S(2)}, u32[]{:S(2)}) async-start(bf16[8,9,3072]{2,1,0:T(8,128)(2,1)} %get-tuple-element.930), calls=%async_computation.7 | async-start | bytes 1572864 | tf_op jit(solution)/shard_map/all_to_all | solution.py:140
  505.9 18.7 %all-to-all-done.7 = bf16[8,9,3072]{2,1,0:T(8,128)(2,1)S(1)} async-done(((bf16[8,9,3072]{2,1,0:T(8,128)(2,1)}), bf16[8,9,3072]{2,1,0:T(8,128)(2,1)S(1)}, u32[]{:S(2)}, u32[]{:S(2)}) %all-to-all-start.7) | async-done | bytes 442400 | tf_op jit(solution)/shard_map/all_to_all | solution.py:140
  538.0 12.7 %collective-permute-done.31 = bf16[12,3072]{1,0:T(8,128)(2,1)S(1)} collective-permute-done((bf16[12,3072]{1,0:T(8,128)(2,1)S(1)}, bf16[12,3072]{1,0:T(8,128)(2,1)S(1)}, u32[]{:S(2)}, u32[]{:S(2)}) %collective-permute-start.31) | collective-permute-done | bytes 73760 | tf_op jit(solution)/shard_map/ppermute | solution.py:35
  563.9 6.1 collective-permute-done.35
  571.0 65.9 %conditional.9 = (bf16[8,9,3072]{2,1,0:T(8,128)(2,1)}, bf16[8,9]{1,0:T(8,128)(2,1)S(1)}) conditional(s32[]{:T(128)} %convert_element_type.389, () %tuple.76, (f32[8,9]{1,0:T(8,128)S(1)}, bf16[8,9,3072]{2,1,0:T(8,128)(2,1)S(1)}, s32[]{:T(128)}, bf16[1,9,3072]{2,1,0:T(8,128)(2,1)S(1)}, s32[]{:T(128)}, /*index=5*/bf16[1,9,3072]{2,1,0:T(8,128)(2,1)S(1)}, ...), branch_computations={%region_31.32_spmd, %region_32.34_spmd} | conditional | flops 9067511808 | bytes 151144912 | solution.py:136
  572.1 10.6 %fusion.141 = f32[72,4096]{1,0:T(8,128)S(1)} fusion(bf16[72,3072]{1,0:T(8,128)(2,1)S(1)} %reshape.337, bf16[3072,4096]{1,0:T(8,128)(2,1)} %get-tuple-element.914), kind=kOutput, calls=%fused_computation.350 | convolution fusion | flops 1811939328 | bytes 26787840 | tf_op jit(solution)/shard_map/cond/branch_1_fun/dot_general | solution.py:57
  584.9 12.5 %fusion.140 = f32[72,4096]{1,0:T(8,128)S(1)} fusion(bf16[72,3072]{1,0:T(8,128)(2,1)} %reshape.336, bf16[4096,3072]{1,0:T(8,128)(2,1)} %get-tuple-element.911), kind=kOutput, calls=%fused_computation.349 | convolution fusion | flops 1811939328 | bytes 26787840 | tf_op jit(solution)/shard_map/cond/branch_1_fun/rd,fd->rf/dot_general | solution.py:59
  597.4 11.2 %multiply_reduce_fusion.4 = (bf16[72]{0:T(256)(128)(2,1)}, f32[72,4096]{1,0:T(8,128)S(1)}) fusion(f32[72,4096]{1,0:T(8,128)S(1)} %fusion.140, f32[72,4096]{1,0:T(8,128)S(1)} %fusion.141, bf16[72,3072]{1,0:T(8,128)(2,1)S(1)} %copy-done.9, bf16[3072,4096]{1,0:T(8,128)(2,1)} %get-tuple-element.913), kind=kOutput, calls=%fused_computation.81 | convolution fusion | flops 1814003584 | bytes 29147280 | tf_op jit(solution)/shard_map/cond/branch_1_fun/dot_general | solution.py:58
  608.7 13.5 %fusion.33 = f32[72,3072]{1,0:T(8,128)} fusion(bf16[3072,4096]{1,0:T(8,128)(2,1)} %get-tuple-element.914, f32[72,4096]{1,0:T(8,128)S(1)} %fusion.141, f32[72,4096]{1,0:T(8,128)S(1)} %get-tuple-element.960, f32[72,4096]{1,0:T(8,128)S(1)} %fusion.140, f32[72]{0:T(128)S(1)} %mul.329), kind=kOutput, calls=%fused_computation.86 | convolution fusion | flops 1815183360 | bytes 29589792 | tf_op jit(solution)/shard_map/cond/branch_1_fun/rf,df->rd/dot_general | solution.py:65
  622.2 13.1 %convolution_add_fusion.4 = bf16[72,3072]{1,0:T(8,128)(2,1)S(1)} fusion(f32[72,3072]{1,0:T(8,128)} %fusion.33, bf16[3072,4096]{1,0:T(8,128)(2,1)} %get-tuple-element.913, f32[72,4096]{1,0:T(8,128)S(1)} %fusion.140, f32[72]{0:T(128)S(1)} %mul.329, f32[72,4096]{1,0:T(8,128)S(1)} %fusion.141), kind=kOutput, calls=%fused_computation.80 | convolution fusion | flops 1814446080 | bytes 28852512 | tf_op jit(solution)/shard_map/cond/branch_1_fun/rf,df->rd/dot_general | solution.py:66
  637.4 6.3 all-to-all-start.14
  644.4 4.9 all-to-all-done.14
  653.4 20.3 %all-to-all-done.9 = bf16[8,9,3072]{2,1,0:T(8,128)(2,1)S(1)} async-done(((bf16[8,9,3072]{2,1,0:T(8,128)(2,1)}), bf16[8,9,3072]{2,1,0:T(8,128)(2,1)S(1)}, u32[]{:S(2)}, u32[]{:S(2)}) %all-to-all-start.9) | async-done | bytes 442400 | tf_op jit(solution)/shard_map/all_to_all | solution.py:140
  (463 shorter events, 187.2 us)
Async XLA Ops:
  5.8 21.2 %collective-permute-start = (bf16[1,9,3072]{2,1,0:T(8,128)(2,1)S(1)}, bf16[1,9,3072]{2,1,0:T(8,128)(2,1)S(1)}, u32[]{:S(2)}, u32[]{:S(2)}) collective-permute-start(bf16[1,9,3072]{2,1,0:T(8,128)(2,1)S(1)} %get-tuple-element.995), channel_id=1, source_target_pairs={{0,1},{1,0},{2,3},{3,2},{4,5},{5,4},{6,7},{7,6},{8,9},{9,8},{10,11... | collective-permute-start | bytes 165896 | tf_op jit(solution)/shard_map/ppermute | solution.py:24
  6.3 24.6 %collective-permute-start.1 = (bf16[1,9,3072]{2,1,0:T(8,128)(2,1)S(1)}, bf16[1,9,3072]{2,1,0:T(8,128)(2,1)S(1)}, u32[]{:S(2)}, u32[]{:S(2)}) collective-permute-start(bf16[1,9,3072]{2,1,0:T(8,128)(2,1)S(1)} %get-tuple-element.994), channel_id=1, source_target_pairs={{0,2},{1,3},{2,0},{3,1},{4,6},{5,7},{6,4},{7,5},{8,10},{9,11},{10,... | collective-permute-start | bytes 165896 | tf_op jit(solution)/shard_map/ppermute | solution.py:24
  8.8 22.8 %collective-permute-start.2 = (bf16[1,9,3072]{2,1,0:T(8,128)(2,1)S(1)}, bf16[1,9,3072]{2,1,0:T(8,128)(2,1)S(1)}, u32[]{:S(2)}, u32[]{:S(2)}) collective-permute-start(bf16[1,9,3072]{2,1,0:T(8,128)(2,1)S(1)} %get-tuple-element.993), channel_id=1, source_target_pairs={{0,3},{1,2},{2,1},{3,0},{4,7},{5,6},{6,5},{7,4},{8,11},{9,10},{10,... | collective-permute-start | bytes 165896 | tf_op jit(solution)/shard_map/ppermute | solution.py:24
  8.9 22.7 %collective-permute-start.3 = (bf16[1,9,3072]{2,1,0:T(8,128)(2,1)S(1)}, bf16[1,9,3072]{2,1,0:T(8,128)(2,1)S(1)}, u32[]{:S(2)}, u32[]{:S(2)}) collective-permute-start(bf16[1,9,3072]{2,1,0:T(8,128)(2,1)S(1)} %get-tuple-element.992), channel_id=1, source_target_pairs={{0,4},{1,5},{2,6},{3,7},{4,0},{5,1},{6,2},{7,3},{8,12},{9,13},{10,... | collective-permute-start | bytes 165896 | tf_op jit(solution)/shard_map/ppermute | solution.py:24
  11.7 20.0 %collective-permute-start.4 = (bf16[1,9,3072]{2,1,0:T(8,128)(2,1)S(1)}, bf16[1,9,3072]{2,1,0:T(8,128)(2,1)S(1)}, u32[]{:S(2)}, u32[]{:S(2)}) collective-permute-start(bf16[1,9,3072]{2,1,0:T(8,128)(2,1)S(1)} %get-tuple-element.991), channel_id=1, source_target_pairs={{0,5},{1,4},{2,7},{3,6},{4,1},{5,0},{6,3},{7,2},{8,13},{9,12},{10,... | collective-permute-start | bytes 165896 | tf_op jit(solution)/shard_map/ppermute | solution.py:24
  14.4 30.7 %all-to-all-start = ((bf16[8,9,3072]{2,1,0:T(8,128)(2,1)}), bf16[8,9,3072]{2,1,0:T(8,128)(2,1)S(1)}, u32[]{:S(2)}, u32[]{:S(2)}) async-start(bf16[8,9,3072]{2,1,0:T(8,128)(2,1)} %bitcast.20), calls=%async_computation | async-start | bytes 1572864 | tf_op jit(solution)/shard_map/all_to_all | solution.py:123
  50.1 26.5 %all-to-all-start.1 = ((bf16[8,9,3072]{2,1,0:T(8,128)(2,1)}), bf16[8,9,3072]{2,1,0:T(8,128)(2,1)S(1)}, u32[]{:S(2)}, u32[]{:S(2)}) async-start(bf16[8,9,3072]{2,1,0:T(8,128)(2,1)} %get-tuple-element.927), calls=%async_computation.1 | async-start | bytes 1572864 | tf_op jit(solution)/shard_map/all_to_all | solution.py:140
  77.6 37.2 %all-to-all-start.2 = ((bf16[8,9,3072]{2,1,0:T(8,128)(2,1)}), bf16[8,9,3072]{2,1,0:T(8,128)(2,1)S(1)}, u32[]{:S(2)}, u32[]{:S(2)}) async-start(bf16[8,9,3072]{2,1,0:T(8,128)(2,1)} %bitcast.35), calls=%async_computation.2 | async-start | bytes 1572864 | tf_op jit(solution)/shard_map/all_to_all | solution.py:123
  91.7 21.5 %collective-permute-start.11 = (bf16[1,9,3072]{2,1,0:T(8,128)(2,1)S(1)}, bf16[1,9,3072]{2,1,0:T(8,128)(2,1)S(1)}, u32[]{:S(2)}, u32[]{:S(2)}) collective-permute-start(bf16[1,9,3072]{2,1,0:T(8,128)(2,1)S(1)} %get-tuple-element.985), channel_id=1, source_target_pairs={{0,4},{1,5},{2,6},{3,7},{4,0},{5,1},{6,2},{7,3},{8,12},{9,13},{10,... | collective-permute-start | bytes 165896 | tf_op jit(solution)/shard_map/ppermute | solution.py:24
  94.3 20.5 %collective-permute-start.12 = (bf16[1,9,3072]{2,1,0:T(8,128)(2,1)S(1)}, bf16[1,9,3072]{2,1,0:T(8,128)(2,1)S(1)}, u32[]{:S(2)}, u32[]{:S(2)}) collective-permute-start(bf16[1,9,3072]{2,1,0:T(8,128)(2,1)S(1)} %get-tuple-element.984), channel_id=1, source_target_pairs={{0,5},{1,4},{2,7},{3,6},{4,1},{5,0},{6,3},{7,2},{8,13},{9,12},{10,... | collective-permute-start | bytes 165896 | tf_op jit(solution)/shard_map/ppermute | solution.py:24
  95.5 19.3 %collective-permute-start.13 = (bf16[1,9,3072]{2,1,0:T(8,128)(2,1)S(1)}, bf16[1,9,3072]{2,1,0:T(8,128)(2,1)S(1)}, u32[]{:S(2)}, u32[]{:S(2)}) collective-permute-start(bf16[1,9,3072]{2,1,0:T(8,128)(2,1)S(1)} %get-tuple-element.983), channel_id=1, source_target_pairs={{0,6},{1,7},{2,4},{3,5},{4,2},{5,3},{6,0},{7,1},{8,14},{9,15},{10,... | collective-permute-start | bytes 165896 | tf_op jit(solution)/shard_map/ppermute | solution.py:24
  97.8 16.9 %collective-permute-start.14 = (bf16[1,9,3072]{2,1,0:T(8,128)(2,1)S(1)}, bf16[1,9,3072]{2,1,0:T(8,128)(2,1)S(1)}, u32[]{:S(2)}, u32[]{:S(2)}) collective-permute-start(bf16[1,9,3072]{2,1,0:T(8,128)(2,1)S(1)} %get-tuple-element.982), channel_id=1, source_target_pairs={{0,7},{1,6},{2,5},{3,4},{4,3},{5,2},{6,1},{7,0},{8,15},{9,14},{10,... | collective-permute-start | bytes 165896 | tf_op jit(solution)/shard_map/ppermute | solution.py:24
  98.6 16.2 %collective-permute-start.8 = (bf16[1,9,3072]{2,1,0:T(8,128)(2,1)S(1)}, bf16[1,9,3072]{2,1,0:T(8,128)(2,1)S(1)}, u32[]{:S(2)}, u32[]{:S(2)}) collective-permute-start(bf16[1,9,3072]{2,1,0:T(8,128)(2,1)S(1)} %get-tuple-element.988), channel_id=1, source_target_pairs={{0,1},{1,0},{2,3},{3,2},{4,5},{5,4},{6,7},{7,6},{8,9},{9,8},{10,11... | collective-permute-start | bytes 165896 | tf_op jit(solution)/shard_map/ppermute | solution.py:24
  122.8 24.6 %all-to-all-start.3 = ((bf16[8,9,3072]{2,1,0:T(8,128)(2,1)}), bf16[8,9,3072]{2,1,0:T(8,128)(2,1)S(1)}, u32[]{:S(2)}, u32[]{:S(2)}) async-start(bf16[8,9,3072]{2,1,0:T(8,128)(2,1)} %get-tuple-element.928), calls=%async_computation.3 | async-start | bytes 1572864 | tf_op jit(solution)/shard_map/all_to_all | solution.py:140
  148.3 26.2 %all-to-all-start.4 = ((bf16[8,9,3072]{2,1,0:T(8,128)(2,1)}), bf16[8,9,3072]{2,1,0:T(8,128)(2,1)S(1)}, u32[]{:S(2)}, u32[]{:S(2)}) async-start(bf16[8,9,3072]{2,1,0:T(8,128)(2,1)} %bitcast.49), calls=%async_computation.4 | async-start | bytes 1572864 | tf_op jit(solution)/shard_map/all_to_all | solution.py:123
  165.0 14.3 %collective-permute-start.18 = (bf16[1,9,3072]{2,1,0:T(8,128)(2,1)S(1)}, bf16[1,9,3072]{2,1,0:T(8,128)(2,1)S(1)}, u32[]{:S(2)}, u32[]{:S(2)}) collective-permute-start(bf16[1,9,3072]{2,1,0:T(8,128)(2,1)S(1)} %get-tuple-element.979), channel_id=1, source_target_pairs={{0,3},{1,2},{2,1},{3,0},{4,7},{5,6},{6,5},{7,4},{8,11},{9,10},{10,... | collective-permute-start | bytes 165896 | tf_op jit(solution)/shard_map/ppermute | solution.py:24
  165.3 18.7 %collective-permute-start.19 = (bf16[1,9,3072]{2,1,0:T(8,128)(2,1)S(1)}, bf16[1,9,3072]{2,1,0:T(8,128)(2,1)S(1)}, u32[]{:S(2)}, u32[]{:S(2)}) collective-permute-start(bf16[1,9,3072]{2,1,0:T(8,128)(2,1)S(1)} %get-tuple-element.978), channel_id=1, source_target_pairs={{0,4},{1,5},{2,6},{3,7},{4,0},{5,1},{6,2},{7,3},{8,12},{9,13},{10,... | collective-permute-start | bytes 165896 | tf_op jit(solution)/shard_map/ppermute | solution.py:24
  167.8 17.1 %collective-permute-start.20 = (bf16[1,9,3072]{2,1,0:T(8,128)(2,1)S(1)}, bf16[1,9,3072]{2,1,0:T(8,128)(2,1)S(1)}, u32[]{:S(2)}, u32[]{:S(2)}) collective-permute-start(bf16[1,9,3072]{2,1,0:T(8,128)(2,1)S(1)} %get-tuple-element.977), channel_id=1, source_target_pairs={{0,5},{1,4},{2,7},{3,6},{4,1},{5,0},{6,3},{7,2},{8,13},{9,12},{10,... | collective-permute-start | bytes 165896 | tf_op jit(solution)/shard_map/ppermute | solution.py:24
  167.8 17.1 %collective-permute-start.21 = (bf16[1,9,3072]{2,1,0:T(8,128)(2,1)S(1)}, bf16[1,9,3072]{2,1,0:T(8,128)(2,1)S(1)}, u32[]{:S(2)}, u32[]{:S(2)}) collective-permute-start(bf16[1,9,3072]{2,1,0:T(8,128)(2,1)S(1)} %get-tuple-element.976), channel_id=1, source_target_pairs={{0,6},{1,7},{2,4},{3,5},{4,2},{5,3},{6,0},{7,1},{8,14},{9,15},{10,... | collective-permute-start | bytes 165896 | tf_op jit(solution)/shard_map/ppermute | solution.py:24
  174.5 15.2 %all-to-all-start.10 = ((bf16[8,1,9]{2,1,0:T(2,128)(2,1)}), bf16[8,1,9]{2,1,0:T(2,128)(2,1)S(1)}, u32[]{:S(2)}, u32[]{:S(2)}) async-start(bf16[8,1,9]{2,1,0:T(2,128)(2,1)} %copy.218), calls=%async_computation.10 | async-start | bytes 8192 | tf_op jit(solution)/shard_map/all_to_all | solution.py:141
  189.7 27.0 %all-to-all-start.5 = ((bf16[8,9,3072]{2,1,0:T(8,128)(2,1)}), bf16[8,9,3072]{2,1,0:T(8,128)(2,1)S(1)}, u32[]{:S(2)}, u32[]{:S(2)}) async-start(bf16[8,9,3072]{2,1,0:T(8,128)(2,1)} %get-tuple-element.929), calls=%async_computation.5 | async-start | bytes 1572864 | tf_op jit(solution)/shard_map/all_to_all | solution.py:140
  221.2 188.2 %collective-permute-start.23 = (bf16[12,3072]{1,0:T(8,128)(2,1)S(1)}, bf16[12,3072]{1,0:T(8,128)(2,1)S(1)}, u32[]{:S(2)}, u32[]{:S(2)}) collective-permute-start(bf16[12,3072]{1,0:T(8,128)(2,1)S(1)} %get-tuple-element.948), channel_id=1, source_target_pairs={{8,0},{16,8},{24,16},{9,1},{17,9},{25,17},{10,2},{18,10},{26,18},{... | collective-permute-start | bytes 221192 | tf_op jit(solution)/shard_map/ppermute | solution.py:35
  226.6 193.0 %all-to-all-start.6 = ((bf16[8,9,3072]{2,1,0:T(8,128)(2,1)}), bf16[8,9,3072]{2,1,0:T(8,128)(2,1)S(1)}, u32[]{:S(2)}, u32[]{:S(2)}) async-start(bf16[8,9,3072]{2,1,0:T(8,128)(2,1)} %bitcast.63), calls=%async_computation.6 | async-start | bytes 1572864 | tf_op jit(solution)/shard_map/all_to_all | solution.py:123
  414.7 14.3 %collective-permute-start.28 = (bf16[1,9,3072]{2,1,0:T(8,128)(2,1)S(1)}, bf16[1,9,3072]{2,1,0:T(8,128)(2,1)S(1)}, u32[]{:S(2)}, u32[]{:S(2)}) collective-permute-start(bf16[1,9,3072]{2,1,0:T(8,128)(2,1)S(1)} %get-tuple-element.970), channel_id=1, source_target_pairs={{0,5},{1,4},{2,7},{3,6},{4,1},{5,0},{6,3},{7,2},{8,13},{9,12},{10,... | collective-permute-start | bytes 165896 | tf_op jit(solution)/shard_map/ppermute | solution.py:24
  419.6 76.8 %all-to-all-start.12 = ((bf16[8,1,9]{2,1,0:T(2,128)(2,1)}), bf16[8,1,9]{2,1,0:T(2,128)(2,1)}, u32[]{:S(2)}, u32[]{:S(2)}) async-start(bf16[8,1,9]{2,1,0:T(2,128)(2,1)} %copy.222), calls=%async_computation.12 | async-start | bytes 8192 | tf_op jit(solution)/shard_map/all_to_all | solution.py:141
  496.4 28.2 %all-to-all-start.7 = ((bf16[8,9,3072]{2,1,0:T(8,128)(2,1)}), bf16[8,9,3072]{2,1,0:T(8,128)(2,1)S(1)}, u32[]{:S(2)}, u32[]{:S(2)}) async-start(bf16[8,9,3072]{2,1,0:T(8,128)(2,1)} %get-tuple-element.930), calls=%async_computation.7 | async-start | bytes 1572864 | tf_op jit(solution)/shard_map/all_to_all | solution.py:140
  529.1 21.6 %collective-permute-start.31 = (bf16[12,3072]{1,0:T(8,128)(2,1)S(1)}, bf16[12,3072]{1,0:T(8,128)(2,1)S(1)}, u32[]{:S(2)}, u32[]{:S(2)}) collective-permute-start(bf16[12,3072]{1,0:T(8,128)(2,1)S(1)} %get-tuple-element.946), channel_id=1, source_target_pairs={{8,0},{16,8},{24,16},{9,1},{17,9},{25,17},{10,2},{18,10},{26,18},{... | collective-permute-start | bytes 221192 | tf_op jit(solution)/shard_map/ppermute | solution.py:35
  534.4 29.5 %all-to-all-start.8 = ((bf16[8,9,3072]{2,1,0:T(8,128)(2,1)}), bf16[8,9,3072]{2,1,0:T(8,128)(2,1)S(1)}, u32[]{:S(2)}, u32[]{:S(2)}) async-start(bf16[8,9,3072]{2,1,0:T(8,128)(2,1)} %bitcast.78), calls=%async_computation.8 | async-start | bytes 1572864 | tf_op jit(solution)/shard_map/all_to_all | solution.py:123
  553.3 16.6 %collective-permute-start.35 = (bf16[1,9,3072]{2,1,0:T(8,128)(2,1)S(1)}, bf16[1,9,3072]{2,1,0:T(8,128)(2,1)S(1)}, u32[]{:S(2)}, u32[]{:S(2)}) collective-permute-start(bf16[1,9,3072]{2,1,0:T(8,128)(2,1)S(1)} %get-tuple-element.964), channel_id=1, source_target_pairs={{0,4},{1,5},{2,6},{3,7},{4,0},{5,1},{6,2},{7,3},{8,12},{9,13},{10,... | collective-permute-start | bytes 165896 | tf_op jit(solution)/shard_map/ppermute | solution.py:24
  555.9 15.0 %collective-permute-start.36 = (bf16[1,9,3072]{2,1,0:T(8,128)(2,1)S(1)}, bf16[1,9,3072]{2,1,0:T(8,128)(2,1)S(1)}, u32[]{:S(2)}, u32[]{:S(2)}) collective-permute-start(bf16[1,9,3072]{2,1,0:T(8,128)(2,1)S(1)} %get-tuple-element.963), channel_id=1, source_target_pairs={{0,5},{1,4},{2,7},{3,6},{4,1},{5,0},{6,3},{7,2},{8,13},{9,12},{10,... | collective-permute-start | bytes 165896 | tf_op jit(solution)/shard_map/ppermute | solution.py:24
  555.9 15.0 %collective-permute-start.37 = (bf16[1,9,3072]{2,1,0:T(8,128)(2,1)S(1)}, bf16[1,9,3072]{2,1,0:T(8,128)(2,1)S(1)}, u32[]{:S(2)}, u32[]{:S(2)}) collective-permute-start(bf16[1,9,3072]{2,1,0:T(8,128)(2,1)S(1)} %get-tuple-element.962), channel_id=1, source_target_pairs={{0,6},{1,7},{2,4},{3,5},{4,2},{5,3},{6,0},{7,1},{8,14},{9,15},{10,... | collective-permute-start | bytes 165896 | tf_op jit(solution)/shard_map/ppermute | solution.py:24
  649.3 24.4 %all-to-all-start.9 = ((bf16[8,9,3072]{2,1,0:T(8,128)(2,1)}), bf16[8,9,3072]{2,1,0:T(8,128)(2,1)S(1)}, u32[]{:S(2)}, u32[]{:S(2)}) async-start(bf16[8,9,3072]{2,1,0:T(8,128)(2,1)} %get-tuple-element.931), calls=%async_computation.9 | async-start | bytes 1572864 | tf_op jit(solution)/shard_map/all_to_all | solution.py:140
  (116 other events, 1606.9 us)
